TPU v7x, 512 devices: a whole 4x8x8 slice. The times are simulated.
512 devices in a mesh: row: 16 (over z, core), col: 32 (over y, x).
Axes of the slice: x: 4, y: 8, z: 8, core: 2. Of those that a mesh axis runs over, the one named last changes fastest.
Arguments:
- initial_voltage: float32 [16, 64, 128, 128], P('row', 'col'), may hold values from -6 to 6
- inject: float32 [16, 64, 128, 128], P('row', 'col'), may hold values from -6 to 6
- conduct: float32 [16, 64, 128, 128], P('row', 'col'), as said below
- capacitance: float32 [16, 64, 128], P('row', 'col'), may hold values from 1 to 4
- track_gain: float32 [16, 64, 2, 32], P('row', 'col'), may hold values from 0.3 to 3
- driver_tile: int32 [16, 32, 64], P('row', 'col'), may hold values from 0 to 1
- sink_net: int32 [16, 32, 32, 8], P('row', 'col'), may hold values from 0 to 63
- sink_count: int32 [16, 32, 32], P('row', 'col'), may hold values from 0 to 8, as said below
- sink_tile: int32 [16, 32, 32, 8], P('row', 'col'), may hold values from 0 to 1
- sink_node: int32 [16, 32, 32, 8], P('row', 'col'), may hold values from 0 to 127
- sink_gain: float32 [16, 32, 32, 8], P('row', 'col'), may hold values from 0.5 to 2
Outputs:
- voltage: float32 [16, 64, 128, 128], P('row', 'col')
Inputs may be any that keep to these rules, and one draw needn't show every extreme that they name: Slots k >= sink_count[d, s] are ignored; some receiving device takes all 8 slots from some source device in every draw. `conduct`: each tile's block is symmetric with non-positive entries off the diagonal and rows summing to zero.
All inputs are finite; a program needn't handle non-finite values.
Results may differ from a plain program's by a relative error of at most 0.0001.
Values sent between devices are 32-bit elements; how exact they have to be, the bound alone decides.
A program may use at most 64 MiB of HBM per device.

v0:
```python
import jax
import jax.numpy as jnp
from jax import lax
from jax.sharding import PartitionSpec as P

ITERS = 3
PRECISE = lax.Precision.HIGHEST


def padded_2(block, sides, width):
    for axis, dim in sides:
        count = lax.axis_size(axis)
        forward = [(i, i + 1) for i in range(count - 1)]
        backward = [(target, source) for source, target in forward]
        low = lax.ppermute(
            lax.slice_in_dim(block, block.shape[dim] - width, None, axis=dim), axis, forward
        )
        high = lax.ppermute(lax.slice_in_dim(block, 0, width, axis=dim), axis, backward)
        block = jnp.concatenate([low, block, high], axis=dim)
    return block


def shifted(block, axis, distance):
    devices = range(lax.axis_size(axis))
    route = [(i - distance, i) for i in devices if i - distance in devices]
    return lax.ppermute(block, axis, route)


def tile_inverse(conduct, capacitance):
    node_count = conduct.shape[-1]
    identity = jnp.eye(node_count, dtype=jnp.float32)
    whole_block = conduct + capacitance[..., None] * identity
    flat_blocks = whole_block.reshape((-1, node_count, node_count))
    factors = jnp.linalg.cholesky(flat_blocks)
    inverse = jax.vmap(lambda factor: jax.scipy.linalg.cho_solve((factor, True), identity))(factors)
    return inverse.reshape(whole_block.shape)


def apply_grid(voltage, conduct, capacitance, track_pad):
    edge_count = track_pad.shape[-1]
    inner_part = (
        jnp.einsum("rcij,rcjp->rcip", conduct, voltage, precision=PRECISE)
        + capacitance[..., None] * voltage
    )
    rim_cells = voltage[:, :, :edge_count, :]
    padded = padded_2(rim_cells, (("row", 0), ("col", 1)), 1)
    east_gain = track_pad[1:-1, 1:-1, 0][..., None]
    west_gain = track_pad[1:-1, :-2, 0][..., None]
    south_gain = track_pad[1:-1, 1:-1, 1][..., None]
    north_gain = track_pad[:-2, 1:-1, 1][..., None]
    track_flow = east_gain * (rim_cells - padded[1:-1, 2:]) + west_gain * (
        rim_cells - padded[1:-1, :-2]
    )
    track_flow = (
        track_flow
        + south_gain * (rim_cells - padded[2:, 1:-1])
        + north_gain * (rim_cells - padded[:-2, 1:-1])
    )
    return jnp.concatenate(
        [inner_part[:, :, :edge_count] + track_flow, inner_part[:, :, edge_count:]], axis=2
    )


def precondition(inverse, residual):
    return jnp.einsum("rcij,rcjp->rcip", inverse, residual, precision=PRECISE)


def inner_sum(left_vec, right_vec):
    return jnp.sum(left_vec * right_vec, axis=(0, 1, 2))


def residual_product(residual, precond):
    return lax.psum(inner_sum(residual, precond), ("row", "col"))


def solve_separate(right_side, initial, conduct, capacitance, track_pad, inverse):
    solution = initial
    residual = right_side - apply_grid(initial, conduct, capacitance, track_pad)
    precond = precondition(inverse, residual)
    direction = precond
    rz_now = residual_product(residual, precond)
    for sweep_idx in range(ITERS):
        applied = apply_grid(direction, conduct, capacitance, track_pad)
        curvature = lax.psum(inner_sum(direction, applied), ("row", "col"))
        step_size = rz_now / curvature
        solution = solution + step_size * direction
        residual = residual - step_size * applied
        precond = precondition(inverse, residual)
        rz_fresh = residual_product(residual, precond)
        direction = precond + rz_fresh / rz_now * direction
        rz_now = rz_fresh
    return solution


def driver_voltage(voltage, driver_tile):
    node_count = voltage.shape[2]
    flat_field = voltage.reshape((-1, voltage.shape[3]))
    net_count = driver_tile.shape[-1]
    row_index = (
        driver_tile.reshape(-1) * node_count + jnp.arange(net_count, dtype=jnp.int32) % node_count
    )
    return jnp.take(flat_field, row_index, axis=0)


def sink_current(values, sink_tile, sink_node, sink_gain, sink_count, node_count, tile_count):
    source_count, slot_count, pattern_count = values.shape
    live_slot = jnp.arange(slot_count, dtype=jnp.int32)[None, :] < sink_count.reshape(
        (source_count, 1)
    )
    weight = jnp.where(live_slot, sink_gain.reshape((source_count, slot_count)), jnp.float32(0.0))
    row_index = (sink_tile * node_count + sink_node).reshape(-1)
    scaled = (values * weight[..., None]).reshape((-1, pattern_count))
    injected = jnp.zeros((tile_count * node_count, pattern_count), jnp.float32)
    return injected.at[row_index].add(scaled)


def lower_rims(track_gain):
    west_piece = shifted(track_gain[:, -1:, 0, :], "col", 1)
    north_piece = shifted(track_gain[-1:, :, 1, :], "row", 1)
    track_pad = jnp.pad(track_gain, ((1, 1), (1, 1), (0, 0), (0, 0)))
    track_pad = track_pad.at[1:-1, 0, 0].set(west_piece[:, 0])
    return track_pad.at[0, 1:-1, 1].set(north_piece[0])


def local(
    initial_voltage,
    inject,
    conduct,
    capacitance,
    track_gain,
    driver_tile,
    sink_net,
    sink_count,
    sink_tile,
    sink_node,
    sink_gain,
):
    inverse = tile_inverse(conduct, capacitance)
    track_pad = lower_rims(track_gain)
    col_count = lax.axis_size("col")
    net_count = driver_tile.shape[-1]
    pattern_count = initial_voltage.shape[3]
    node_count = initial_voltage.shape[2]
    tile_count = initial_voltage.shape[0] * initial_voltage.shape[1]
    wanted = sink_net.reshape((sink_net.shape[2], sink_net.shape[3]))
    voltage = initial_voltage
    drivers = driver_voltage(voltage, driver_tile)
    gathered = lax.all_gather(drivers, "col", axis=0, tiled=True)
    offsets = jnp.arange(col_count, dtype=jnp.int32)[:, None] * net_count
    values = jnp.take(gathered, (wanted + offsets).reshape(-1), axis=0).reshape(
        wanted.shape + (pattern_count,)
    )
    injected = sink_current(
        values, sink_tile, sink_node, sink_gain, sink_count, node_count, tile_count
    )
    right_side = capacitance[..., None] * voltage + inject + injected.reshape(voltage.shape)
    voltage = solve_separate(right_side, voltage, conduct, capacitance, track_pad, inverse)
    return voltage


def solution(mesh):
    placed = (
        P("row", "col", None, None),
        P("row", "col", None, None),
        P("row", "col", None, None),
        P("row", "col", None),
        P("row", "col", None, None),
        P("row", "col", None),
        P("row", "col", None, None),
        P("row", "col", None),
        P("row", "col", None, None),
        P("row", "col", None, None),
        P("row", "col", None, None),
    )
    return jax.shard_map(
        local, mesh=mesh, in_specs=placed, out_specs=P("row", "col", None, None), check_vma=False
    )
```

profile of v0, /device:TPU:1, one launch (start us, length us, event | category | flops | bytes accessed | tf_op | source)
XLA Modules:
  0.0 707.5 jit_solution(17942465035946714458)
XLA Ops:
  6.5 1.1 copy.150
  7.6 8.8 %collective-permute-start.2 = (f32[1,2,32,128]{2,3,1,0:T(8,128)S(1)}, f32[1,2,32,128]{2,3,1,0:T(8,128)S(1)}, u32[]{:S(2)}, u32[]{:S(2)}) collective-permute-start(f32[1,2,32,128]{2,3,1,0:T(8,128)S(1)} %bitcast.150), channel_id=1, source_target_pairs={{32,0},{64,32},{96,64},{128,96},{160,128},{192,160},{224,192},{256... | collective-permute-start | bytes 98312 | tf_op jit(solution)/shard_map/ppermute | solution.py:18
  16.4 1.9 collective-permute-start.1
  18.4 1.3 collective-permute-start
  19.7 1.9 collective-permute-start.5
  21.7 0.6 gather_fusion
  22.3 0.7 broadcast_select_fusion
  23.3 0.6 copy-done.5
  24.2 0.6 copy-done.9
  25.0 0.5 copy-done.6
  25.7 0.6 copy-done.8
  26.5 0.7 copy-done.3
  28.0 0.8 copy-done.2
  29.1 1.3 collective-permute-start.3
  30.4 4.0 collective-permute-start.4
  34.5 1.1 collective-permute-done.4
  35.9 66.4 %all-gather.2.cloned.1.call-done = f32[2048,128]{1,0:T(8,128)} async-done(((f32[64,128]{1,0:T(8,128)}), f32[2048,128]{1,0:T(8,128)}) %all-gather.2.cloned.1.call-update) | async-done | bytes 1048592 | tf_op jit(solution)/shard_map/all_gather | solution.py:148
  102.3 3.4 scatter_custom_fusion
  106.0 23.5 %custom-call.11 = f32[2,128,128]{2,1,0:T(8,128)S(1)} custom-call(f32[2,128,128]{2,1,0:T(8,128)S(1)} %fusion.13), custom_call_target="Cholesky" | custom-call | tf_op jit(solution)/shard_map/jit(cholesky)/cholesky | solution.py:34
  129.8 19.7 %custom-call.12 = f32[2,1,128,128]{2,3,1,0:T(8,128)S(1)} custom-call(f32[2,1,128,128]{3,2,1,0:T(8,128)S(1)} %select_bitcast_fusion), custom_call_target="InvertDiagBlocksLowerTriangular" | custom-call | tf_op jit(solution)/shard_map/vmap(jit(_cho_solve))/triangular_solve | solution.py:35
  151.0 6.9 collective-permute-start.7
  157.9 3.2 collective-permute-start.6
  161.3 0.5 collective-permute-done.7
  161.9 1.2 collective-permute-done.6
  163.1 1.3 collective-permute-start.8
  164.4 4.0 collective-permute-start.9
  168.6 1.0 collective-permute-done.9
  170.1 103.8 %all-reduce.1 = (f32[128]{0:T(128)S(1)}, f32[128]{0:T(128)S(1)}) all-reduce(f32[128]{0:T(128)S(1)} %multiply_reduce_fusion, f32[128]{0:T(128)S(1)} %fusion.8), channel_id=1, replica_groups=mesh['row'=16,'col'=32] {'row','col'}, use_global_device_ids=true, to_apply=%region_4.5 | all-reduce | flops 256 | bytes 2048 | tf_op jit(solution)/shard_map/psum | solution.py:73
  274.0 0.5 fusion.17
  274.5 95.4 %psum.44 = f32[128]{0:T(128)S(1)} all-reduce(f32[128]{0:T(128)S(1)} %get-tuple-element.56), channel_id=1, replica_groups=mesh['row'=16,'col'=32] {'row','col'}, use_global_device_ids=true, to_apply=%region_8.9 | all-reduce | flops 128 | bytes 1024 | tf_op jit(solution)/shard_map/psum | solution.py:73
  370.0 2.6 collective-permute-start.11
  372.6 3.3 collective-permute-start.10
  375.9 0.4 fusion.3
  376.7 1.2 collective-permute-done.10
  377.9 1.3 collective-permute-start.12
  379.2 4.0 collective-permute-start.13
  383.3 1.0 collective-permute-done.13
  384.8 102.0 %psum.45 = f32[128]{0:T(128)S(1)} all-reduce(f32[128]{0:T(128)S(1)} %fusion.10), channel_id=1, replica_groups=mesh['row'=16,'col'=32] {'row','col'}, use_global_device_ids=true, to_apply=%region_10.11 | all-reduce | flops 128 | bytes 1024 | tf_op jit(solution)/shard_map/psum | solution.py:84
  486.8 0.5 fusion.14
  487.4 95.3 %psum.46 = f32[128]{0:T(128)S(1)} all-reduce(f32[128]{0:T(128)S(1)} %get-tuple-element.58), channel_id=1, replica_groups=mesh['row'=16,'col'=32] {'row','col'}, use_global_device_ids=true, to_apply=%region_12.13 | all-reduce | flops 128 | bytes 1024 | tf_op jit(solution)/shard_map/psum | solution.py:73
  582.7 2.6 collective-permute-start.15
  585.3 3.5 collective-permute-start.14
  589.6 1.2 collective-permute-done.14
  590.8 1.3 collective-permute-start.16
  592.1 4.0 collective-permute-start.17
  596.2 1.0 collective-permute-done.17
  597.8 102.0 %psum.47 = f32[128]{0:T(128)S(1)} all-reduce(f32[128]{0:T(128)S(1)} %fusion.12), channel_id=1, replica_groups=mesh['row'=16,'col'=32] {'row','col'}, use_global_device_ids=true, to_apply=%region_14.15 | all-reduce | flops 128 | bytes 1024 | tf_op jit(solution)/shard_map/psum | solution.py:84
  699.9 0.8 copy.172
  (128 shorter events, 8.3 us)
Async XLA Ops:
  6.5 15.1 %copy-start.1 = (f32[1,2,128,128]{3,2,1,0:T(8,128)S(1)}, f32[1,2,128,128]{3,2,1,0:T(8,128)}, u32[]{:S(2)}) copy-start(f32[1,2,128,128]{3,2,1,0:T(8,128)} %param.15) | copy-start | bytes 393220
  6.5 11.8 %copy-start.4 = (f32[1,2,2,32]{3,2,1,0:T(2,128)S(1)}, f32[1,2,2,32]{3,2,1,0:T(2,128)}, u32[]{:S(2)}) copy-start(f32[1,2,2,32]{3,2,1,0:T(2,128)} %param.19) | copy-start | bytes 1540
  6.5 95.8 %all-gather.2.cloned.1.call-start = ((), (), s32[]{:S(2)}) async-start(), calls=%async_computation | async-start | bytes 1081344 | tf_op jit(solution)/shard_map/all_gather | solution.py:148
  7.6 21.3 %collective-permute-start.2 = (f32[1,2,32,128]{2,3,1,0:T(8,128)S(1)}, f32[1,2,32,128]{2,3,1,0:T(8,128)S(1)}, u32[]{:S(2)}, u32[]{:S(2)}) collective-permute-start(f32[1,2,32,128]{2,3,1,0:T(8,128)S(1)} %bitcast.150), channel_id=1, source_target_pairs={{32,0},{64,32},{96,64},{128,96},{160,128},{192,160},{224,192},{256... | collective-permute-start | bytes 98312 | tf_op jit(solution)/shard_map/ppermute | solution.py:18
  16.4 12.6 %collective-permute-start.1 = (f32[1,2,32,128]{2,3,1,0:T(8,128)S(1)}, f32[1,2,32,128]{2,3,1,0:T(8,128)S(1)}, u32[]{:S(2)}, u32[]{:S(2)}) collective-permute-start(f32[1,2,32,128]{2,3,1,0:T(8,128)S(1)} %bitcast.151), channel_id=1, source_target_pairs={{0,32},{32,64},{64,96},{96,128},{128,160},{160,192},{192,224},{224... | collective-permute-start | bytes 98312 | tf_op jit(solution)/shard_map/ppermute | solution.py:15
  18.4 10.5 %collective-permute-start = (f32[1,1,32]{2,1,0:T(1,128)S(1)}, f32[1,1,32]{2,1,0:T(1,128)S(1)}, u32[]{:S(2)}, u32[]{:S(2)}) collective-permute-start(f32[1,1,32]{2,1,0:T(1,128)S(1)} %slice_bitcast_fusion.1), channel_id=1, source_target_pairs={{0,1},{1,2},{2,3},{3,4},{4,5},{5,6},{6,7},{7,8},{8,9},{9,10},{10,1... | collective-permute-start | bytes 392 | tf_op jit(solution)/shard_map/ppermute | solution.py:26
  19.7 1.9 copy-start.10
  19.7 16.1 %collective-permute-start.5 = (f32[1,2,32]{2,1,0:T(2,128)S(1)}, f32[1,2,32]{2,1,0:T(2,128)S(1)}, u32[]{:S(2)}, u32[]{:S(2)}) collective-permute-start(f32[1,2,32]{2,1,0:T(2,128)S(1)} %bitcast.184), channel_id=1, source_target_pairs={{0,32},{32,64},{64,96},{96,128},{128,160},{160,192},{192,224},{224... | collective-permute-start | bytes 776 | tf_op jit(solution)/shard_map/ppermute | solution.py:26
  23.2 0.7 copy-start.5
  23.8 2.7 copy-start
  24.1 0.7 copy-start.9
  24.8 0.7 copy-start.6
  24.8 0.7 copy-start.7
  25.6 0.7 copy-start.8
  26.5 0.7 copy-start.3
  27.9 0.9 copy-start.2
  29.1 5.3 collective-permute-start.3
  30.4 5.2 collective-permute-start.4
  151.0 10.8 %collective-permute-start.7 = (f32[1,2,32,128]{2,3,1,0:T(8,128)S(1)}, f32[1,2,32,128]{2,3,1,0:T(8,128)S(1)}, u32[]{:S(2)}, u32[]{:S(2)}) collective-permute-start(f32[1,2,32,128]{2,3,1,0:T(8,128)S(1)} %bitcast.142), channel_id=1, source_target_pairs={{32,0},{64,32},{96,64},{128,96},{160,128},{192,160},{224,192},{256... | collective-permute-start | bytes 98312 | tf_op jit(solution)/shard_map/ppermute | solution.py:18
  157.9 5.1 collective-permute-start.6
  163.1 5.4 collective-permute-start.8
  164.4 5.2 collective-permute-start.9
  370.0 6.6 collective-permute-start.11
  372.6 5.2 collective-permute-start.10
  377.9 5.4 collective-permute-start.12
  379.2 5.2 collective-permute-start.13
  582.7 6.8 collective-permute-start.15
  585.3 5.4 collective-permute-start.14
  590.8 5.4 collective-permute-start.16
  592.1 5.2 collective-permute-start.17
Sparse Core Ops, SparseCore 0:
  23.1 79.1 all-gather.1
where the time goes:
time: 709 us; the launch traced here: 707 us
  blocking collectives  498 us (70%)
  waiting for transfers between devices  75.2 us (11%)
  starting transfers between devices  57 us (8%)
  other arithmetic  49.2 us (7%)
  between operations  14.1 us (2%)
  local copies, waits for them, and re-layouts  9.8 us (1%)
    psum x3, blocking collectives, residual_product(): return lax.psum(inner_sum(residual, precond), ('row', 'col'))  295 us
    psum x2, blocking collectives, solve_separate(): curvature = lax.psum(inner_sum(direction, applied), ('row', 'col'))  204 us
    all_gather x1, waiting for transfers between devices, local(): gathered = lax.all_gather(drivers, 'col', axis=0, tiled=True)  66.4 us
    ppermute x8, starting transfers between devices, padded_2(): lax.ppermute(lax.slice_in_dim(block, block.shape[dim] - width, None, axis...  27.8 us
    ppermute x8, starting transfers between devices, padded_2(): lax.ppermute(lax.slice_in_dim(block, 0, width, axis=dim), axis, backward)  26 us
    another operation x4, other arithmetic, tile_inverse(): factors = jnp.linalg.cholesky(flat_blocks)  23.6 us
    another operation x3, other arithmetic, tile_inverse(): jax.scipy.linalg.cho_solve((factor, True), identity)  19.8 us
  transfers between devices with their start and end apart: 19, of which 11 were waited for; matrix products, arithmetic and copies ran while one was open for 1% of the time, Pallas kernels for 0%

commit v1 on v0

--- a/solution.py
+++ b/solution.py
@@ -145,7 +145,10 @@
     wanted = sink_net.reshape((sink_net.shape[2], sink_net.shape[3]))
     voltage = initial_voltage
     drivers = driver_voltage(voltage, driver_tile)
-    gathered = lax.all_gather(drivers, "col", axis=0, tiled=True)
+    size = lax.axis_size("col")
+    parts = jnp.stack([drivers for _ in range(size)])
+    parts = lax.all_to_all(parts, "col", split_axis=0, concat_axis=0)
+    gathered = jnp.concatenate(parts, axis=0)
     offsets = jnp.arange(col_count, dtype=jnp.int32)[:, None] * net_count
     values = jnp.take(gathered, (wanted + offsets).reshape(-1), axis=0).reshape(
         wanted.shape + (pattern_count,)

time: 709 us -> 655 us (0.924)
  waiting for transfers between devices: 75.2 us -> 29.7 us
  between operations: 14.1 us -> 0.77 us
    all_gather x1 -> x0, waiting for transfers between devices: 66.4 us -> none  [local(): gathered = lax.all_gather(drivers, 'col', axis=0, tiled=True)]
    all_to_all x0 -> x1, waiting for transfers between devices: none -> 13.5 us  [local(): parts = lax.all_to_all(parts, 'col', split_axis=0, concat_axis=0)]
    ppermute x8, waiting for transfers between devices: 1.06 us -> 11.5 us  [padded_2(): lax.ppermute(lax.slice_in_dim(block, 0, width, axis=dim), axis, backward)]
    ppermute x8, starting transfers between devices: 26 us -> 15.6 us  [padded_2(): lax.ppermute(lax.slice_in_dim(block, 0, width, axis=dim), axis, backward)]
    all_to_all x0 -> x1, starting transfers between devices: none -> 9.38 us  [local(): parts = lax.all_to_all(parts, 'col', split_axis=0, concat_axis=0)]
  transfers between devices with their start and end apart: 19 -> 19, of which waited for: 11 -> 9; matrix products, arithmetic and copies ran while one was open for 1% -> 1% of each run, Pallas kernels for 0% -> 0%
where the time goes in v1:
time: 655 us; the launch traced here: 654 us
  blocking collectives  497 us (76%)
  starting transfers between devices  63.5 us (10%)
  other arithmetic  47.6 us (7%)
  waiting for transfers between devices  29.7 us (5%)
  local copies, waits for them, and re-layouts  11 us (2%)
    psum x3, blocking collectives, residual_product(): return lax.psum(inner_sum(residual, precond), ('row', 'col'))  296 us
    psum x2, blocking collectives, solve_separate(): curvature = lax.psum(inner_sum(direction, applied), ('row', 'col'))  202 us
    ppermute x8, starting transfers between devices, padded_2(): lax.ppermute(lax.slice_in_dim(block, block.shape[dim] - width, None, axis...  34.2 us
    another operation x4, other arithmetic, tile_inverse(): factors = jnp.linalg.cholesky(flat_blocks)  23.6 us
    another operation x3, other arithmetic, tile_inverse(): jax.scipy.linalg.cho_solve((factor, True), identity)  19.8 us
    ppermute x8, starting transfers between devices, padded_2(): lax.ppermute(lax.slice_in_dim(block, 0, width, axis=dim), axis, backward)  15.6 us
    all_to_all x1, waiting for transfers between devices, local(): parts = lax.all_to_all(parts, 'col', split_axis=0, concat_axis=0)  13.5 us
  transfers between devices with their start and end apart: 19, of which 9 were waited for; matrix products, arithmetic and copies ran while one was open for 1% of the time, Pallas kernels for 0%

profile of v1, /device:TPU:1, one launch (start us, length us, event | category | flops | bytes accessed | tf_op | source)
XLA Modules:
  0.0 653.6 jit_solution(14563105003955530149)
XLA Ops:
  0.0 1.1 copy.150
  1.1 5.4 collective-permute-start.1
  6.5 4.7 collective-permute-start.2
  11.2 1.3 collective-permute-start
  12.5 3.0 collective-permute-start.5
  15.6 0.6 gather_fusion
  16.2 1.1 stack.2
  17.3 9.4 %all-to-all-start = ((f32[32,64,128]{2,1,0:T(8,128)}), f32[32,64,128]{2,1,0:T(8,128)S(1)}, u32[]{:S(2)}, u32[]{:S(2)}) async-start(f32[32,64,128]{2,1,0:T(8,128)} %stack.2), calls=%async_computation | async-start | bytes 2097152 | tf_op jit(solution)/shard_map/all_to_all | solution.py:150
  27.0 0.6 copy-done.5
  27.9 0.7 copy-done.6
  28.7 0.6 copy-done.9
  29.5 0.5 copy-done.7
  30.3 0.7 copy-done.3
  31.8 0.8 copy-done.2
  33.0 1.3 collective-permute-start.3
  34.3 4.0 collective-permute-start.4
  38.4 1.7 collective-permute-done.4
  40.4 13.5 %all-to-all-done = f32[32,64,128]{2,1,0:T(8,128)S(1)} async-done(((f32[32,64,128]{2,1,0:T(8,128)}), f32[32,64,128]{2,1,0:T(8,128)S(1)}, u32[]{:S(2)}, u32[]{:S(2)}) %all-to-all-start) | async-done | bytes 1048608 | tf_op jit(solution)/shard_map/all_to_all | solution.py:150
  54.0 2.4 scatter_custom_fusion
  56.7 23.5 %custom-call.11 = f32[2,128,128]{2,1,0:T(8,128)S(1)} custom-call(f32[2,128,128]{2,1,0:T(8,128)S(1)} %fusion.13), custom_call_target="Cholesky" | custom-call | tf_op jit(solution)/shard_map/jit(cholesky)/cholesky | solution.py:34
  80.4 19.7 %custom-call.12 = f32[2,1,128,128]{2,3,1,0:T(8,128)S(1)} custom-call(f32[2,1,128,128]{3,2,1,0:T(8,128)S(1)} %select_bitcast_fusion), custom_call_target="InvertDiagBlocksLowerTriangular" | custom-call | tf_op jit(solution)/shard_map/vmap(jit(_cho_solve))/triangular_solve | solution.py:35
  101.3 4.1 collective-permute-start.6
  105.4 1.9 collective-permute-start.7
  108.0 3.7 collective-permute-done.7
  111.8 1.3 collective-permute-start.8
  113.1 4.2 collective-permute-start.9
  117.4 0.9 collective-permute-done.9
  118.7 105.2 %all-reduce.1 = (f32[128]{0:T(128)S(1)}, f32[128]{0:T(128)S(1)}) all-reduce(f32[128]{0:T(128)S(1)} %multiply_reduce_fusion, f32[128]{0:T(128)S(1)} %fusion.8), channel_id=1, replica_groups=mesh['row'=16,'col'=32] {'row','col'}, use_global_device_ids=true, to_apply=%region_4.5 | all-reduce | flops 256 | bytes 2048 | tf_op jit(solution)/shard_map/psum | solution.py:73
  224.0 0.5 fusion.17
  224.5 95.4 %psum.44 = f32[128]{0:T(128)S(1)} all-reduce(f32[128]{0:T(128)S(1)} %get-tuple-element.56), channel_id=1, replica_groups=mesh['row'=16,'col'=32] {'row','col'}, use_global_device_ids=true, to_apply=%region_8.9 | all-reduce | flops 128 | bytes 1024 | tf_op jit(solution)/shard_map/psum | solution.py:73
  320.0 4.2 collective-permute-start.10
  324.2 1.9 collective-permute-start.11
  326.7 3.8 collective-permute-done.11
  330.6 1.3 collective-permute-start.12
  331.9 4.0 collective-permute-start.13
  336.0 1.0 collective-permute-done.13
  337.5 100.8 %psum.45 = f32[128]{0:T(128)S(1)} all-reduce(f32[128]{0:T(128)S(1)} %fusion.10), channel_id=1, replica_groups=mesh['row'=16,'col'=32] {'row','col'}, use_global_device_ids=true, to_apply=%region_10.11 | all-reduce | flops 128 | bytes 1024 | tf_op jit(solution)/shard_map/psum | solution.py:84
  438.3 0.5 fusion.14
  438.8 95.3 %psum.46 = f32[128]{0:T(128)S(1)} all-reduce(f32[128]{0:T(128)S(1)} %get-tuple-element.58), channel_id=1, replica_groups=mesh['row'=16,'col'=32] {'row','col'}, use_global_device_ids=true, to_apply=%region_12.13 | all-reduce | flops 128 | bytes 1024 | tf_op jit(solution)/shard_map/psum | solution.py:73
  534.2 4.4 collective-permute-start.14
  538.6 1.9 collective-permute-start.15
  540.5 0.4 fusion.5
  541.1 3.8 collective-permute-done.15
  545.0 1.3 collective-permute-start.16
  546.3 4.0 collective-permute-start.17
  550.4 1.0 collective-permute-done.17
  551.9 100.8 %psum.47 = f32[128]{0:T(128)S(1)} all-reduce(f32[128]{0:T(128)S(1)} %fusion.12), channel_id=1, replica_groups=mesh['row'=16,'col'=32] {'row','col'}, use_global_device_ids=true, to_apply=%region_14.15 | all-reduce | flops 128 | bytes 1024 | tf_op jit(solution)/shard_map/psum | solution.py:84
  652.8 0.8 copy.172
  (128 shorter events, 8.1 us)
Async XLA Ops:
  0.0 15.6 %copy-start.1 = (f32[1,2,128,128]{3,2,1,0:T(8,128)S(1)}, f32[1,2,128,128]{3,2,1,0:T(8,128)}, u32[]{:S(2)}) copy-start(f32[1,2,128,128]{3,2,1,0:T(8,128)} %param.15) | copy-start | bytes 393220
  0.0 11.2 %copy-start.4 = (f32[1,2,2,32]{3,2,1,0:T(2,128)S(1)}, f32[1,2,2,32]{3,2,1,0:T(2,128)}, u32[]{:S(2)}) copy-start(f32[1,2,2,32]{3,2,1,0:T(2,128)} %param.19) | copy-start | bytes 1540
  1.1 31.7 %collective-permute-start.1 = (f32[1,2,32,128]{2,3,1,0:T(8,128)S(1)}, f32[1,2,32,128]{2,3,1,0:T(8,128)S(1)}, u32[]{:S(2)}, u32[]{:S(2)}) collective-permute-start(f32[1,2,32,128]{2,3,1,0:T(8,128)S(1)} %bitcast.151), channel_id=1, source_target_pairs={{0,32},{32,64},{64,96},{96,128},{128,160},{160,192},{192,224},{224... | collective-permute-start | bytes 98312 | tf_op jit(solution)/shard_map/ppermute | solution.py:15
  6.5 26.4 %collective-permute-start.2 = (f32[1,2,32,128]{2,3,1,0:T(8,128)S(1)}, f32[1,2,32,128]{2,3,1,0:T(8,128)S(1)}, u32[]{:S(2)}, u32[]{:S(2)}) collective-permute-start(f32[1,2,32,128]{2,3,1,0:T(8,128)S(1)} %bitcast.152), channel_id=1, source_target_pairs={{32,0},{64,32},{96,64},{128,96},{160,128},{192,160},{224,192},{256... | collective-permute-start | bytes 98312 | tf_op jit(solution)/shard_map/ppermute | solution.py:18
  11.2 21.5 %collective-permute-start = (f32[1,1,32]{2,1,0:T(1,128)S(1)}, f32[1,1,32]{2,1,0:T(1,128)S(1)}, u32[]{:S(2)}, u32[]{:S(2)}) collective-permute-start(f32[1,1,32]{2,1,0:T(1,128)S(1)} %slice_bitcast_fusion.1), channel_id=1, source_target_pairs={{0,1},{1,2},{2,3},{3,4},{4,5},{5,6},{6,7},{7,8},{8,9},{9,10},{10,1... | collective-permute-start | bytes 392 | tf_op jit(solution)/shard_map/ppermute | solution.py:26
  12.5 3.0 copy-start.10
  12.5 27.8 %collective-permute-start.5 = (f32[1,2,32]{2,1,0:T(2,128)S(1)}, f32[1,2,32]{2,1,0:T(2,128)S(1)}, u32[]{:S(2)}, u32[]{:S(2)}) collective-permute-start(f32[1,2,32]{2,1,0:T(2,128)S(1)} %bitcast.186), channel_id=1, source_target_pairs={{0,32},{32,64},{64,96},{96,128},{128,160},{160,192},{192,224},{224... | collective-permute-start | bytes 776 | tf_op jit(solution)/shard_map/ppermute | solution.py:26
  17.3 36.6 %all-to-all-start = ((f32[32,64,128]{2,1,0:T(8,128)}), f32[32,64,128]{2,1,0:T(8,128)S(1)}, u32[]{:S(2)}, u32[]{:S(2)}) async-start(f32[32,64,128]{2,1,0:T(8,128)} %stack.2), calls=%async_computation | async-start | bytes 2097152 | tf_op jit(solution)/shard_map/all_to_all | solution.py:150
  26.9 0.7 copy-start.5
  27.6 2.8 copy-start
  27.9 0.7 copy-start.6
  28.7 0.7 copy-start.9
  29.4 0.7 copy-start.7
  29.4 0.7 copy-start.8
  30.3 0.7 copy-start.3
  31.7 0.9 copy-start.2
  33.0 5.5 collective-permute-start.3
  34.3 5.9 collective-permute-start.4
  101.3 6.6 %collective-permute-start.6 = (f32[1,2,32,128]{2,3,1,0:T(8,128)S(1)}, f32[1,2,32,128]{2,3,1,0:T(8,128)S(1)}, u32[]{:S(2)}, u32[]{:S(2)}) collective-permute-start(f32[1,2,32,128]{2,3,1,0:T(8,128)S(1)} %bitcast.143), channel_id=1, source_target_pairs={{0,32},{32,64},{64,96},{96,128},{128,160},{160,192},{192,224},{224... | collective-permute-start | bytes 98312 | tf_op jit(solution)/shard_map/ppermute | solution.py:15
  105.4 6.3 collective-permute-start.7
  111.8 5.6 collective-permute-start.8
  113.1 5.2 collective-permute-start.9
  320.0 6.6 %collective-permute-start.10 = (f32[1,2,32,128]{2,3,1,0:T(8,128)S(1)}, f32[1,2,32,128]{2,3,1,0:T(8,128)S(1)}, u32[]{:S(2)}, u32[]{:S(2)}) collective-permute-start(f32[1,2,32,128]{2,3,1,0:T(8,128)S(1)} %bitcast.147), channel_id=1, source_target_pairs={{0,32},{32,64},{64,96},{96,128},{128,160},{160,192},{192,224},{224... | collective-permute-start | bytes 98312 | tf_op jit(solution)/shard_map/ppermute | solution.py:15
  324.2 6.3 collective-permute-start.11
  330.6 5.4 collective-permute-start.12
  331.9 5.2 collective-permute-start.13
  534.2 6.8 %collective-permute-start.14 = (f32[1,2,32,128]{2,3,1,0:T(8,128)S(1)}, f32[1,2,32,128]{2,3,1,0:T(8,128)S(1)}, u32[]{:S(2)}, u32[]{:S(2)}) collective-permute-start(f32[1,2,32,128]{2,3,1,0:T(8,128)S(1)} %bitcast.154), channel_id=1, source_target_pairs={{0,32},{32,64},{64,96},{96,128},{128,160},{160,192},{192,224},{224... | collective-permute-start | bytes 98312 | tf_op jit(solution)/shard_map/ppermute | solution.py:15
  538.6 6.3 collective-permute-start.15
  545.0 5.4 collective-permute-start.16
  546.3 5.2 collective-permute-start.17
